TPU v7x, 512 devices: a whole 4x8x8 slice. The times are simulated.
512 devices in a mesh: pix: 32 (over x, y), tm: 16 (over z, core).
Axes of the slice: x: 4, y: 8, z: 8, core: 2. Of those that a mesh axis runs over, the one named last changes fastest.
Arguments:
- movie_frames: bfloat16 [128, 1024, 4096], P('tm', 'pix'), may hold values from -48 to 48
- depth_index: int32 [1024], P('pix'), may hold values from 0 to 5
- depth_width: float32 [6], replicated, may hold values from 0.7 to 3
- temporal_test_matrix: float32 [128, 96], replicated, may hold values from -4 to 4
- merge_probe: float32 [192, 96], replicated, may hold values from -4 to 4
Outputs:
- temporal_rows: float32 [96, 128], P(None, 'tm')
- loadings: bfloat16 [96, 1024, 4096], P(None, 'pix', 'tm')
All inputs are finite; a program needn't handle non-finite values.
Results may differ from a plain program's by a relative error of at most 0.0062.
Values may be sent and summed in bfloat16 or wider, within the bound.
No kernel may reach another device: no remote copies, remote signals or barrier semaphores. Data moves between devices by JAX's collectives and lax.ppermute only.
A program may use at most 64 MiB of HBM per device.

v0:
```python
import math
import jax
import jax.numpy as jnp
from jax import lax
from jax.sharding import PartitionSpec as P

ROWS_DEV = 32
COLS = 4096
HW = 4
NDEPTH = 6
greatest_rank = lax.Precision.HIGHEST
reduction_multiplier = math.sqrt(0.5)
growth_multiplier = math.sqrt(2.0)


def with_halo(block, sides, width):
    for axis, dim in sides:
        count = lax.axis_size(axis)
        forward = [(i, i + 1) for i in range(count - 1)]
        backward = [(target, source) for source, target in forward]
        low = lax.ppermute(
            lax.slice_in_dim(block, block.shape[dim] - width, None, axis=dim), axis, forward
        )
        high = lax.ppermute(lax.slice_in_dim(block, 0, width, axis=dim), axis, backward)
        block = jnp.concatenate([low, block, high], axis=dim)
    return block


def partner_2(value, axis, distance):
    mask = 2**distance
    pairs = [(source, source ^ mask) for source in range(lax.axis_size(axis))]
    return lax.ppermute(value, axis, pairs)


def taps_table(depth_width):
    offsets = jnp.arange(-HW, HW + 1).astype(jnp.float32)
    kernel_raw = jnp.exp(-offsets[None, :] ** 2 / (2.0 * depth_width[:, None] ** 2))
    return kernel_raw / jnp.sum(kernel_raw, axis=1, keepdims=True)


def row_weights(row_depth, depth_width):
    classes = jnp.arange(NDEPTH)
    onehot = (row_depth[:, None] == classes[None, :]).astype(jnp.float32)
    return jnp.dot(onehot, taps_table(depth_width), precision=greatest_rank)


def smooth_rows(padded, weights):
    row_count = weights.shape[0]
    summed = jnp.zeros((padded.shape[0], row_count, padded.shape[2]), jnp.float32)
    for offset in range(2 * HW + 1):
        summed = summed + weights[:, offset][None, :, None] * padded[
            :, offset : offset + row_count, :
        ].astype(jnp.float32)
    return summed.astype(jnp.bfloat16)


def orthonormal(sketch):
    factor = jnp.linalg.cholesky(jnp.dot(sketch.T, sketch, precision=greatest_rank))
    return lax.linalg.triangular_solve(
        factor, sketch, left_side=False, lower=True, transpose_a=True
    )


def tile_basis(scatter_matrix, temporal_test_matrix):
    basis_cols = orthonormal(jnp.dot(scatter_matrix, temporal_test_matrix, precision=greatest_rank))
    projected = jnp.dot(basis_cols.T, scatter_matrix, precision=greatest_rank)
    inner_gram = jnp.dot(projected, basis_cols, precision=greatest_rank)
    factor = jnp.linalg.cholesky(inner_gram)
    coefficient = lax.linalg.triangular_solve(
        factor, basis_cols, left_side=False, lower=True, transpose_a=True
    )
    return (factor, projected, coefficient)


def body(movie_frames, depth_index, depth_width, temporal_test_matrix, merge_probe):
    weights = row_weights(depth_index, depth_width)
    padded = with_halo(movie_frames, (("pix", 1),), HW)
    smoothed = smooth_rows(padded, weights)
    columns = lax.all_to_all(smoothed, "tm", split_axis=2, concat_axis=0, tiled=True)
    frame_total = columns.shape[0]
    flattened = columns.reshape(frame_total, -1)
    partial_cov = lax.dot_general(
        flattened, flattened, (((1,), (1,)), ((), ())), preferred_element_type=jnp.float32
    )
    scatter_matrix = lax.psum(partial_cov, "tm") / (ROWS_DEV * COLS)
    factor, projected, coefficient = tile_basis(scatter_matrix, temporal_test_matrix)
    span_length = movie_frames.shape[0]
    span_start = lax.axis_index("tm") * span_length
    rank_count = projected.shape[0]
    tree_level_count = lax.axis_size("pix").bit_length() - 1
    pix_position = lax.axis_index("pix")
    path_product = jnp.eye(rank_count, dtype=jnp.float32)
    own_projected = lax.dynamic_slice_in_dim(projected, span_start, span_length, 1)
    own_rows = lax.linalg.triangular_solve(factor, own_projected, left_side=True, lower=True)
    for merge_level in range(tree_level_count):
        partner = partner_2(own_rows, "pix", merge_level)
        is_first = pix_position >> merge_level & 1 == 0
        first_rows = jnp.where(is_first, own_rows, partner)
        second_rows = jnp.where(is_first, partner, own_rows)
        stacked = jnp.concatenate([first_rows, second_rows], axis=0)
        stacked_gram = lax.psum(jnp.dot(stacked, stacked.T, precision=greatest_rank), "tm")
        rotation = orthonormal(jnp.dot(stacked_gram, merge_probe, precision=greatest_rank))
        own_rows = jnp.dot(rotation.T, stacked, precision=greatest_rank) * reduction_multiplier
        rotation_block = (
            jnp.where(is_first, rotation[:rank_count], rotation[rank_count:]) * growth_multiplier
        )
        path_product = jnp.dot(path_product, rotation_block, precision=greatest_rank)
    weights_table = jnp.dot(coefficient, path_product, precision=greatest_rank).astype(jnp.bfloat16)
    loading_flat = lax.dot_general(
        weights_table, flattened, (((0,), (0,)), ((), ())), preferred_element_type=jnp.float32
    )
    loadings = loading_flat.astype(jnp.bfloat16).reshape(
        rank_count, columns.shape[1], columns.shape[2]
    )
    return (own_rows, loadings)


def solution(mesh):
    in_specs = (P("tm", "pix", None), P("pix"), P(), P(), P())
    out_specs = (P(None, "tm"), P(None, "pix", "tm"))
    return jax.shard_map(body, mesh=mesh, in_specs=in_specs, out_specs=out_specs, check_vma=False)
```

profile of v0, /device:TPU:1, one launch (start us, length us, event | category | flops | bytes accessed | tf_op | source)
XLA Modules:
  0.0 986.0 jit_solution(14767062543887843147)
XLA Ops:
  25.3 9.2 copy.75
  34.5 13.4 %reshape.80 = bf16[16,2,32768]{2,1,0:T(2,128)(2,1)S(1)} reshape(bf16[4096,8,32]{2,1,0:T(8,128)(2,1)} %bitcast.158) | data formatting | bytes 4194304
  47.9 64.5 %all_to_all.15 = bf16[16,2,32768]{2,1,0:T(2,128)(2,1)} all-to-all(bf16[16,2,32768]{2,1,0:T(2,128)(2,1)S(1)} %reshape.80), channel_id=1, replica_groups=mesh['pix'=32,'tm'=16] {'tm'}, dimensions={0} | all-to-all | bytes 4194304 | tf_op jit(solution)/shard_map/all_to_all | solution.py:79
  112.4 12.9 %reshape.81 = bf16[4096,8,32]{2,1,0:T(8,128)(2,1)} reshape(bf16[16,2,32768]{2,1,0:T(2,128)(2,1)} %all_to_all.15) | data formatting | bytes 4194304
  125.3 8.8 copy.86
  135.9 105.2 %all-reduce.7.cloned.1.call-done = f32[128,128]{1,0:T(8,128)} async-done(((f32[128,128]{1,0:T(8,128)}), f32[128,128]{1,0:T(8,128)}) %all-reduce.7.cloned.1.call-update) | async-done | bytes 65552 | tf_op jit(solution)/shard_map/psum | solution.py:85
  242.5 8.8 cholesky.119
  252.6 7.4 custom-call.17
  261.6 8.8 cholesky.130
  271.7 7.4 custom-call.11
  285.5 110.7 %all-reduce.9.cloned.1.call-done = f32[192,192]{1,0:T(8,128)} async-done(((f32[192,192]{1,0:T(8,128)}), f32[192,192]{1,0:T(8,128)}) %all-reduce.9.cloned.1.call-update) | async-done | bytes 147472 | tf_op jit(solution)/shard_map/psum | solution.py:101
  397.9 8.8 cholesky.141
  408.0 7.4 custom-call.18
  422.4 113.0 %all-reduce.11.cloned.1.call-done = f32[192,192]{1,0:T(8,128)} async-done(((f32[192,192]{1,0:T(8,128)}), f32[192,192]{1,0:T(8,128)}) %all-reduce.11.cloned.1.call-update) | async-done | bytes 147472 | tf_op jit(solution)/shard_map/psum | solution.py:101
  537.1 8.8 cholesky.152
  547.2 7.4 custom-call.19
  565.1 112.5 %all-reduce.13.cloned.1.call-done = f32[192,192]{1,0:T(8,128)} async-done(((f32[192,192]{1,0:T(8,128)}), f32[192,192]{1,0:T(8,128)}) %all-reduce.13.cloned.1.call-update) | async-done | bytes 147472 | tf_op jit(solution)/shard_map/psum | solution.py:101
  679.3 8.8 cholesky.163
  703.3 112.7 %all-reduce.15.cloned.1.call-done = f32[192,192]{1,0:T(8,128)} async-done(((f32[192,192]{1,0:T(8,128)}), f32[192,192]{1,0:T(8,128)}) %all-reduce.15.cloned.1.call-update) | async-done | bytes 147472 | tf_op jit(solution)/shard_map/psum | solution.py:101
  817.7 8.8 cholesky.174
  827.8 7.4 custom-call.21
  843.1 112.7 %all-reduce.17.cloned.1.call-done = f32[192,192]{1,0:T(8,128)} async-done(((f32[192,192]{1,0:T(8,128)}), f32[192,192]{1,0:T(8,128)}) %all-reduce.17.cloned.1.call-update) | async-done | bytes 147472 | tf_op jit(solution)/shard_map/psum | solution.py:101
  957.5 8.8 cholesky.185
  967.6 7.4 custom-call.22
  (130 shorter events, 89.9 us)
Async XLA Ops:
  7.2 389.0 %copy-start = (f32[192,96]{1,0:T(8,128)S(1)}, f32[192,96]{1,0:T(8,128)}, u32[]{:S(2)}) copy-start(f32[192,96]{1,0:T(8,128)} %param.14) | copy-start | bytes 221188
  7.2 11.8 %copy-start.1 = (bf16[8,32,4096]{2,1,0:T(8,128)(2,1)S(1)}, bf16[8,32,4096]{2,1,0:T(8,128)(2,1)}, u32[]{:S(2)}) copy-start(bf16[8,32,4096]{2,1,0:T(8,128)(2,1)} %param.10) | copy-start | bytes 6291460
  7.2 9.7 copy-start.3
  7.2 9.9 %copy-start.4 = (s32[32]{0:T(128)S(1)}, s32[32]{0:T(128)}, u32[]{:S(2)}) copy-start(s32[32]{0:T(128)} %param.11) | copy-start | bytes 388
  7.2 233.9 %all-reduce.7.cloned.1.call-start = ((), (), s32[]{:S(2)}) async-start(), calls=%async_computation.1 | async-start | bytes 131072 | tf_op jit(solution)/shard_map/psum | solution.py:85
  9.0 9.6 collective-permute-start.1
  10.5 8.0 collective-permute-start
  134.2 106.9 %copy-start.2 = (f32[128,96]{0,1:T(8,128)S(1)}, f32[128,96]{0,1:T(8,128)}, u32[]{:S(2)}) copy-start(f32[128,96]{0,1:T(8,128)} %param.13) | copy-start | bytes 147460
  135.5 260.6 %all-reduce.9.cloned.1.call-start = ((), (), s32[]{:S(2)}) async-start(), calls=%async_computation.2 | async-start | bytes 393216 | tf_op jit(solution)/shard_map/psum | solution.py:101
  279.4 4.4 collective-permute-start.2
  284.9 250.5 %all-reduce.11.cloned.1.call-start = ((), (), s32[]{:S(2)}) async-start(), calls=%async_computation.3 | async-start | bytes 393216 | tf_op jit(solution)/shard_map/psum | solution.py:101
  415.9 5.3 collective-permute-start.3
  422.3 255.3 %all-reduce.13.cloned.1.call-start = ((), (), s32[]{:S(2)}) async-start(), calls=%async_computation.4 | async-start | bytes 393216 | tf_op jit(solution)/shard_map/psum | solution.py:101
  555.1 8.3 collective-permute-start.4
  564.6 251.4 %all-reduce.15.cloned.1.call-start = ((), (), s32[]{:S(2)}) async-start(), calls=%async_computation.5 | async-start | bytes 393216 | tf_op jit(solution)/shard_map/psum | solution.py:101
  697.4 4.4 collective-permute-start.5
  702.9 252.9 %all-reduce.17.cloned.1.call-start = ((), (), s32[]{:S(2)}) async-start(), calls=%async_computation.6 | async-start | bytes 393216 | tf_op jit(solution)/shard_map/psum | solution.py:101
  835.7 5.9 collective-permute-start.6
Sparse Core Ops, SparseCore 0:
  135.7 105.3 all-reduce.6
  285.0 111.0 all-reduce.8
  422.5 112.8 all-reduce.10
  564.7 112.8 all-reduce.12
  703.0 112.8 all-reduce.14
  842.9 112.8 all-reduce.16
where the time goes:
time: 992 us; the launch traced here: 986 us
  waiting for transfers between devices  673 us (68%)
  other arithmetic  129 us (13%)
  blocking collectives  64.5 us (7%)
  local copies, waits for them, and re-layouts  50.7 us (5%)
  starting transfers between devices  29.5 us (3%)
  matrix products  24.3 us (2%)
  between operations  15 us (2%)
    psum x5, waiting for transfers between devices, body(): lax.psum(jnp.dot(stacked, stacked.T, precision=greatest_rank), 'tm')  562 us
    psum x1, waiting for transfers between devices, body(): scatter_matrix = lax.psum(partial_cov, 'tm') / (ROWS_DEV * COLS)  105 us
    all_to_all x1, blocking collectives, body(): lax.all_to_all(smoothed, 'tm', split_axis=2, concat_axis=0, tiled=True)  64.5 us
    another operation x18, other arithmetic, orthonormal(): jnp.linalg.cholesky(jnp.dot(sketch.T, sketch, precision=greatest_rank))  56.7 us
    another operation x12, other arithmetic, orthonormal(): lax.linalg.triangular_solve(factor, sketch, left_side=False, lower=True,...  48.1 us
    unnamed x17, local copies, waits for them, and re-layouts  38.8 us
    ppermute x5, starting transfers between devices, partner_2(): return lax.ppermute(value, axis, pairs)  22.3 us
  transfers between devices with their start and end apart: 13, of which 12 were waited for; matrix products, arithmetic and copies ran while one was open for 0% of the time, Pallas kernels for 0%

commit v1 on v0

--- a/solution.py
+++ b/solution.py
@@ -82,7 +82,10 @@
     partial_cov = lax.dot_general(
         flattened, flattened, (((1,), (1,)), ((), ())), preferred_element_type=jnp.float32
     )
-    scatter_matrix = lax.psum(partial_cov, "tm") / (ROWS_DEV * COLS)
+    supply_all_the_cubes = lambda raw, ax_name: jax.lax.all_gather(raw, axis_name=ax_name).sum(
+        axis=0
+    )
+    scatter_matrix = supply_all_the_cubes(partial_cov, "tm") / (ROWS_DEV * COLS)
     factor, projected, coefficient = tile_basis(scatter_matrix, temporal_test_matrix)
     span_length = movie_frames.shape[0]
     span_start = lax.axis_index("tm") * span_length

time: 992 us -> 927 us (0.934)
  waiting for transfers between devices: 673 us -> 609 us
    psum x1 -> x0, waiting for transfers between devices: 105 us -> none  [body(): scatter_matrix = lax.psum(partial_cov, 'tm') / (ROWS_DEV * COLS)]
    all_gather x0 -> x1, waiting for transfers between devices: none -> 40.9 us  [body(): jax.lax.all_gather(raw, axis_name=ax_name).sum(axis=0)]
where the time goes in v1:
time: 927 us; the launch traced here: 921 us
  waiting for transfers between devices  609 us (66%)
  other arithmetic  130 us (14%)
  blocking collectives  64.5 us (7%)
  local copies, waits for them, and re-layouts  50.7 us (5%)
  starting transfers between devices  29.5 us (3%)
  matrix products  22.6 us (2%)
  between operations  15 us (2%)
    psum x5, waiting for transfers between devices, body(): lax.psum(jnp.dot(stacked, stacked.T, precision=greatest_rank), 'tm')  561 us
    all_to_all x1, blocking collectives, body(): lax.all_to_all(smoothed, 'tm', split_axis=2, concat_axis=0, tiled=True)  64.5 us
    another operation x18, other arithmetic, orthonormal(): jnp.linalg.cholesky(jnp.dot(sketch.T, sketch, precision=greatest_rank))  56.7 us
    another operation x12, other arithmetic, orthonormal(): lax.linalg.triangular_solve(factor, sketch, left_side=False, lower=True,...  48.1 us
    all_gather x1, waiting for transfers between devices, body(): jax.lax.all_gather(raw, axis_name=ax_name).sum(axis=0)  40.9 us
    unnamed x17, local copies, waits for them, and re-layouts  38.8 us
    ppermute x5, starting transfers between devices, partner_2(): return lax.ppermute(value, axis, pairs)  22.3 us
  transfers between devices with their start and end apart: 13, of which 12 were waited for; matrix products, arithmetic and copies ran while one was open for 0% of the time, Pallas kernels for 0%

profile of v1, /device:TPU:1, one launch (start us, length us, event | category | flops | bytes accessed | tf_op | source)
XLA Modules:
  0.0 921.2 jit_solution(603261771021720269)
XLA Ops:
  25.3 9.2 copy.75
  34.5 13.4 %reshape.81 = bf16[16,2,32768]{2,1,0:T(2,128)(2,1)S(1)} reshape(bf16[4096,8,32]{2,1,0:T(8,128)(2,1)} %bitcast.159) | data formatting | bytes 4194304
  47.9 64.5 %all_to_all.15 = bf16[16,2,32768]{2,1,0:T(2,128)(2,1)} all-to-all(bf16[16,2,32768]{2,1,0:T(2,128)(2,1)S(1)} %reshape.81), channel_id=1, replica_groups=mesh['pix'=32,'tm'=16] {'tm'}, dimensions={0} | all-to-all | bytes 4194304 | tf_op jit(solution)/shard_map/all_to_all | solution.py:79
  112.4 12.9 %reshape.82 = bf16[4096,8,32]{2,1,0:T(8,128)(2,1)} reshape(bf16[16,2,32768]{2,1,0:T(2,128)(2,1)} %all_to_all.15) | data formatting | bytes 4194304
  125.3 8.8 copy.86
  135.9 40.9 %all-gather.3.cloned.1.call-done = f32[2048,128]{1,0:T(8,128)} async-done(((f32[128,128]{1,0:T(8,128)}), f32[2048,128]{1,0:T(8,128)}) %all-gather.3.cloned.1.call-update) | async-done | bytes 1048592 | tf_op jit(solution)/shard_map/all_gather | solution.py:85
  178.6 8.8 cholesky.119
  188.7 7.4 custom-call.17
  196.9 8.8 cholesky.130
  207.0 7.4 custom-call.11
  220.8 110.6 %all-reduce.6.cloned.1.call-done = f32[192,192]{1,0:T(8,128)} async-done(((f32[192,192]{1,0:T(8,128)}), f32[192,192]{1,0:T(8,128)}) %all-reduce.6.cloned.1.call-update) | async-done | bytes 147472 | tf_op jit(solution)/shard_map/psum | solution.py:104
  333.1 8.8 cholesky.141
  343.2 7.4 custom-call.18
  357.6 113.0 %all-reduce.8.cloned.1.call-done = f32[192,192]{1,0:T(8,128)} async-done(((f32[192,192]{1,0:T(8,128)}), f32[192,192]{1,0:T(8,128)}) %all-reduce.8.cloned.1.call-update) | async-done | bytes 147472 | tf_op jit(solution)/shard_map/psum | solution.py:104
  472.3 8.8 cholesky.152
  482.4 7.4 custom-call.19
  500.3 112.5 %all-reduce.10.cloned.1.call-done = f32[192,192]{1,0:T(8,128)} async-done(((f32[192,192]{1,0:T(8,128)}), f32[192,192]{1,0:T(8,128)}) %all-reduce.10.cloned.1.call-update) | async-done | bytes 147472 | tf_op jit(solution)/shard_map/psum | solution.py:104
  614.6 8.8 cholesky.163
  624.7 7.4 custom-call.20
  638.5 112.7 %all-reduce.12.cloned.1.call-done = f32[192,192]{1,0:T(8,128)} async-done(((f32[192,192]{1,0:T(8,128)}), f32[192,192]{1,0:T(8,128)}) %all-reduce.12.cloned.1.call-update) | async-done | bytes 147472 | tf_op jit(solution)/shard_map/psum | solution.py:104
  752.9 8.8 cholesky.174
  763.0 7.4 custom-call.21
  778.3 112.7 %all-reduce.14.cloned.1.call-done = f32[192,192]{1,0:T(8,128)} async-done(((f32[192,192]{1,0:T(8,128)}), f32[192,192]{1,0:T(8,128)}) %all-reduce.14.cloned.1.call-update) | async-done | bytes 147472 | tf_op jit(solution)/shard_map/psum | solution.py:104
  892.7 8.8 cholesky.185
  (131 shorter events, 89.5 us)
Async XLA Ops:
  7.2 324.2 %copy-start = (f32[192,96]{1,0:T(8,128)S(1)}, f32[192,96]{1,0:T(8,128)}, u32[]{:S(2)}) copy-start(f32[192,96]{1,0:T(8,128)} %param.14) | copy-start | bytes 221188
  7.2 11.8 %copy-start.1 = (bf16[8,32,4096]{2,1,0:T(8,128)(2,1)S(1)}, bf16[8,32,4096]{2,1,0:T(8,128)(2,1)}, u32[]{:S(2)}) copy-start(bf16[8,32,4096]{2,1,0:T(8,128)(2,1)} %param.10) | copy-start | bytes 6291460
  7.2 9.7 %copy-start.3 = (f32[6]{0:T(128)S(1)}, f32[6]{0:T(128)}, u32[]{:S(2)}) copy-start(f32[6]{0:T(128)} %param.12) | copy-start | bytes 76
  7.2 9.9 %copy-start.4 = (s32[32]{0:T(128)S(1)}, s32[32]{0:T(128)}, u32[]{:S(2)}) copy-start(s32[32]{0:T(128)} %param.11) | copy-start | bytes 388
  7.2 169.5 %all-gather.3.cloned.1.call-start = ((), (), s32[]{:S(2)}) async-start(), calls=%async_computation.6 | async-start | bytes 1114112 | tf_op jit(solution)/shard_map/all_gather | solution.py:85
  9.0 9.6 %collective-permute-start.1 = (bf16[8,4,4096]{2,0,1:T(8,128)(2,1)S(1)}, bf16[8,4,4096]{2,0,1:T(8,128)(2,1)S(1)}, u32[]{:S(2)}, u32[]{:S(2)}) collective-permute-start(bf16[8,4,4096]{2,0,1:T(8,128)(2,1)S(1)} %copy.85), channel_id=1, source_target_pairs={{16,0},{32,16},{48,32},{64,48},{80,64},{96,80},{112,96},{128,112},... | collective-permute-start | bytes 786440 | tf_op jit(solution)/shard_map/ppermute | solution.py:24
  10.5 8.0 collective-permute-start
  134.2 43.9 %copy-start.2 = (f32[128,96]{0,1:T(8,128)S(1)}, f32[128,96]{0,1:T(8,128)}, u32[]{:S(2)}) copy-start(f32[128,96]{0,1:T(8,128)} %param.13) | copy-start | bytes 147460
  135.5 195.8 %all-reduce.6.cloned.1.call-start = ((), (), s32[]{:S(2)}) async-start(), calls=%async_computation.1 | async-start | bytes 393216 | tf_op jit(solution)/shard_map/psum | solution.py:104
  214.7 4.4 collective-permute-start.2
  220.2 250.4 %all-reduce.8.cloned.1.call-start = ((), (), s32[]{:S(2)}) async-start(), calls=%async_computation.2 | async-start | bytes 393216 | tf_op jit(solution)/shard_map/psum | solution.py:104
  351.1 5.3 collective-permute-start.3
  357.6 255.3 %all-reduce.10.cloned.1.call-start = ((), (), s32[]{:S(2)}) async-start(), calls=%async_computation.3 | async-start | bytes 393216 | tf_op jit(solution)/shard_map/psum | solution.py:104
  490.4 8.3 collective-permute-start.4
  499.8 251.3 %all-reduce.12.cloned.1.call-start = ((), (), s32[]{:S(2)}) async-start(), calls=%async_computation.4 | async-start | bytes 393216 | tf_op jit(solution)/shard_map/psum | solution.py:104
  632.6 4.4 collective-permute-start.5
  638.1 252.8 %all-reduce.14.cloned.1.call-start = ((), (), s32[]{:S(2)}) async-start(), calls=%async_computation.5 | async-start | bytes 393216 | tf_op jit(solution)/shard_map/psum | solution.py:104
  770.9 5.9 collective-permute-start.6
Sparse Core Ops, SparseCore 0:
  135.7 41.0 all-gather.2
  220.3 110.9 all-reduce.5
  357.7 112.8 all-reduce.7
  499.9 112.8 all-reduce.9
  638.2 112.8 all-reduce.11
  778.1 112.8 all-reduce.13
